TPU v7x, 32 devices: a whole 2x2x4 slice. The times are simulated.
32 devices in a mesh: group: 2 (over y), row: 8 (over z, x), col: 2 (over core).
Axes of the slice: x: 2, y: 2, z: 4, core: 2. Of those that a mesh axis runs over, the one named last changes fastest.
Arguments:
- map_in: bfloat16 [192, 96, 48], P(('group', 'row'), 'col'), parts along dimension 0, may hold values from -6 to 6
- embedding: bfloat16 [192, 96], P(('group', 'row')), parts along dimension 0, may hold values from -6 to 6
- w_row: bfloat16 [96, 48], replicated, may hold values from -0.625 to 0.625
- w_col: bfloat16 [96, 48], replicated, may hold values from -0.625 to 0.625
- first_kernel_weight: bfloat16 [3, 3, 48, 48], replicated, may hold values from -0.3125 to 0.3125
- first_bias: float32 [48], replicated, may hold values from -0.5 to 0.5
- second_kernel_weight: bfloat16 [3, 3, 48, 48], replicated, may hold values from -0.3125 to 0.3125
- second_bias: float32 [48], replicated, may hold values from -0.5 to 0.5
- w_mix: bfloat16 [48, 48], replicated, may hold values from -0.875 to 0.875
- b_mix: float32 [48], replicated, may hold values from -0.5 to 0.5
- w_head: float32 [48], replicated, may hold values from -0.875 to 0.875
Outputs:
- contacts: float32 [192, 96], P(('group', 'row'), 'col'), parts along dimension 0
There are 2 independent parts, one for each index of `group`. A program takes and returns all parts, laid end to end along the dimension named above; an argument that names none is the same for every part. Nothing has to cross between parts.
All inputs are finite; a program needn't handle non-finite values.
Results may differ from a plain program's by a relative error of at most 0.0055.
Values may be sent and summed in bfloat16 or wider, within the bound.
A program may use at most 64 MiB of HBM per device.

v0:
```python
import jax
import jax.numpy as jnp
from jax import lax
from jax.sharding import PartitionSpec as P

FIRST_DILATION = 4
SECOND_DILATION = 8


def padded(array, sides, width):
    for axis, dim in sides:
        peers, length = (lax.axis_size(axis), array.shape[dim])
        up = [(i, (i + 1) % peers) for i in range(peers - 1)]
        down = [(j, i) for i, j in up]
        last = lax.slice_in_dim(array, length - width, length, axis=dim)
        leading = lax.slice_in_dim(array, 0, width, axis=dim)
        before = lax.ppermute(last, axis, up)
        after = lax.ppermute(leading, axis, down)
        array = jnp.concatenate([before, array, after], axis=dim)
    return array


def swapped(value, axis, bit):
    mask = 2**bit
    pairs = [(source, source ^ mask) for source in range(lax.axis_size(axis))]
    return lax.ppermute(value, axis, pairs)


def dilated_conv(active, weight, spacing, out_rows, out_cols):
    windows = []
    for tap_row in range(3):
        for tap_col in range(3):
            windows.append(
                active[
                    tap_row * spacing : tap_row * spacing + out_rows,
                    tap_col * spacing : tap_col * spacing + out_cols,
                ]
            )
    stacked = jnp.concatenate(windows, axis=-1)
    flat_weight = weight.reshape(9 * weight.shape[2], weight.shape[3])
    return jnp.einsum("rch,hk->rck", stacked, flat_weight, preferred_element_type=jnp.float32)


def on_device(
    map_in,
    embedding,
    w_row,
    w_col,
    first_kernel_weight,
    first_bias,
    second_kernel_weight,
    second_bias,
    w_mix,
    b_mix,
    w_head,
):
    patch_rows, patch_columns, channels = map_in.shape
    row_count = lax.axis_size("row")
    row_at = lax.axis_index("row")
    col_at = lax.axis_index("col")
    all_bins = lax.all_gather(embedding, "row", axis=0, tiled=True)
    row_terms = jnp.dot(all_bins, w_row, preferred_element_type=jnp.float32)
    col_terms = jnp.dot(all_bins, w_col, preferred_element_type=jnp.float32)
    own_rows = lax.dynamic_slice_in_dim(row_terms, row_at * patch_rows, patch_rows, 0)
    own_cols = lax.dynamic_slice_in_dim(col_terms, col_at * patch_columns, patch_columns, 0)
    contact_grid = (
        map_in.astype(jnp.float32) + own_rows[:, None, :] + own_cols[None, :, :]
    ).astype(jnp.bfloat16)
    first_padded = padded(contact_grid, (("row", 0), ("col", 1)), FIRST_DILATION)
    first_layer = (
        contact_grid.astype(jnp.float32)
        + dilated_conv(
            jnp.maximum(first_padded, 0),
            first_kernel_weight,
            FIRST_DILATION,
            patch_rows,
            patch_columns,
        )
        + first_bias
    ).astype(jnp.bfloat16)
    second_padded = padded(first_layer, (("row", 0), ("col", 1)), SECOND_DILATION)
    second_layer = (
        first_layer.astype(jnp.float32)
        + dilated_conv(
            jnp.maximum(second_padded, 0),
            second_kernel_weight,
            SECOND_DILATION,
            patch_rows,
            patch_columns,
        )
        + second_bias
    ).astype(jnp.bfloat16)
    half_rows = patch_rows // 2
    blocks_per = row_count // 2
    arranged = second_layer.reshape(2, half_rows, blocks_per, patch_rows, channels)
    arranged = arranged.transpose(0, 2, 1, 3, 4).reshape(
        2 * blocks_per, half_rows, patch_rows, channels
    )
    exchanged = lax.all_to_all(
        lax.all_to_all(arranged, "row", split_axis=0, concat_axis=0, tiled=True),
        "col",
        split_axis=0,
        concat_axis=0,
        tiled=True,
    )
    exchanged = exchanged.reshape(2, blocks_per, half_rows, patch_rows, channels)
    top_half = row_at // blocks_per
    kept_part = lax.dynamic_index_in_dim(exchanged, top_half, 0, keepdims=False)
    sent_part = lax.dynamic_index_in_dim(exchanged, 1 - top_half, 0, keepdims=False)
    came_back = swapped(sent_part, "row", blocks_per.bit_length() - 1)
    stacked = jnp.where(
        top_half == 0, jnp.stack([kept_part, came_back]), jnp.stack([came_back, kept_part])
    )
    mirrored = stacked.transpose(3, 1, 0, 2, 4).reshape(patch_rows, patch_columns, channels)
    symmetric = ((second_layer.astype(jnp.float32) + mirrored.astype(jnp.float32)) * 0.5).astype(
        jnp.bfloat16
    )
    mixture = (
        jnp.einsum("rch,hk->rck", symmetric, w_mix, preferred_element_type=jnp.float32) + b_mix
    )
    mixture = jnp.maximum(mixture, 0.0)
    return jnp.sum(mixture * w_head, axis=-1)


def solution(mesh):
    placed = (
        P(("group", "row"), "col", None),
        P(("group", "row"), None),
        P(),
        P(),
        P(),
        P(),
        P(),
        P(),
        P(),
        P(),
        P(),
    )
    return jax.shard_map(
        on_device, mesh=mesh, in_specs=placed, out_specs=P(("group", "row"), "col"), check_vma=False
    )
```

profile of v0, /device:TPU:0, one launch (start us, length us, event | category | flops | bytes accessed | tf_op | source)
XLA Modules:
  0.0 92.6 jit_solution(15328792908924847365)
XLA Ops:
  0.0 0.7 copy-done.5
  0.7 32.3 %all-gather = bf16[8,12,96]{2,1,0:T(8,128)(2,1)S(1)} all-gather(bf16[1,12,96]{2,1,0:T(8,128)(2,1)S(1)} %bitcast.32), channel_id=1, replica_groups=mesh['group'=2,'row'=8,'col'=2] {'row'}, dimensions={0}, use_global_device_ids=true | all-gather | bytes 20736 | tf_op jit(solution)/shard_map/all_gather | solution.py:61
  34.0 3.4 %collective-permute-start = (bf16[4,48,48]{2,1,0:T(8,128)(2,1)S(1)}, bf16[4,48,48]{2,1,0:T(8,128)(2,1)S(1)}, u32[]{:S(2)}, u32[]{:S(2)}) collective-permute-start(bf16[4,48,48]{2,1,0:T(8,128)(2,1)S(1)} %get-tuple-element.31), channel_id=1, source_target_pairs={{0,2},{2,4},{4,6},{6,8},{8,10},{10,12},{12,14},{1,3},{3,5},{5,7},{... | collective-permute-start | bytes 55304 | tf_op jit(solution)/shard_map/ppermute | solution.py:17
  37.4 1.3 %collective-permute-start.1 = (bf16[4,48,48]{2,1,0:T(8,128)(2,1)S(1)}, bf16[4,48,48]{2,1,0:T(8,128)(2,1)S(1)}, u32[]{:S(2)}, u32[]{:S(2)}) collective-permute-start(bf16[4,48,48]{2,1,0:T(8,128)(2,1)S(1)} %get-tuple-element.32), channel_id=1, source_target_pairs={{2,0},{4,2},{6,4},{8,6},{10,8},{12,10},{14,12},{3,1},{5,3},{7,5},{... | collective-permute-start | bytes 55304 | tf_op jit(solution)/shard_map/ppermute | solution.py:18
  39.2 4.3 %collective-permute-done.1 = bf16[4,48,48]{2,1,0:T(8,128)(2,1)S(1)} collective-permute-done((bf16[4,48,48]{2,1,0:T(8,128)(2,1)S(1)}, bf16[4,48,48]{2,1,0:T(8,128)(2,1)S(1)}, u32[]{:S(2)}, u32[]{:S(2)}) %collective-permute-start.1) | collective-permute-done | bytes 18464 | tf_op jit(solution)/shard_map/ppermute | solution.py:18
  43.4 1.3 %collective-permute-start.2 = (bf16[20,4,48]{2,1,0:T(4,128)(2,1)S(1)}, bf16[20,4,48]{2,1,0:T(4,128)(2,1)S(1)}, u32[]{:S(2)}, u32[]{:S(2)}) collective-permute-start(bf16[20,4,48]{2,1,0:T(4,128)(2,1)S(1)} %get-tuple-element.25), channel_id=1, source_target_pairs={{0,1},{2,3},{4,5},{6,7},{8,9},{10,11},{12,13},{14,15},{16,17},{18,... | collective-permute-start | bytes 23048 | tf_op jit(solution)/shard_map/ppermute | solution.py:17
  44.7 1.3 %collective-permute-start.3 = (bf16[20,4,48]{2,1,0:T(4,128)(2,1)S(1)}, bf16[20,4,48]{2,1,0:T(4,128)(2,1)S(1)}, u32[]{:S(2)}, u32[]{:S(2)}) collective-permute-start(bf16[20,4,48]{2,1,0:T(4,128)(2,1)S(1)} %get-tuple-element.26), channel_id=1, source_target_pairs={{1,0},{3,2},{5,4},{7,6},{9,8},{11,10},{13,12},{15,14},{17,16},{19,... | collective-permute-start | bytes 23048 | tf_op jit(solution)/shard_map/ppermute | solution.py:18
  46.0 1.8 %collective-permute-done.3 = bf16[20,4,48]{2,1,0:T(4,128)(2,1)S(1)} collective-permute-done((bf16[20,4,48]{2,1,0:T(4,128)(2,1)S(1)}, bf16[20,4,48]{2,1,0:T(4,128)(2,1)S(1)}, u32[]{:S(2)}, u32[]{:S(2)}) %collective-permute-start.3) | collective-permute-done | bytes 7712 | tf_op jit(solution)/shard_map/ppermute | solution.py:18
  48.2 0.6 concatenate.20
  48.8 0.6 copy-done.6
  49.8 2.8 %collective-permute-start.4 = (bf16[8,48,48]{2,1,0:T(8,128)(2,1)S(1)}, bf16[8,48,48]{2,1,0:T(8,128)(2,1)S(1)}, u32[]{:S(2)}, u32[]{:S(2)}) collective-permute-start(bf16[8,48,48]{2,1,0:T(8,128)(2,1)S(1)} %get-tuple-element.29), channel_id=1, source_target_pairs={{0,2},{2,4},{4,6},{6,8},{8,10},{10,12},{12,14},{1,3},{3,5},{5,7},{... | collective-permute-start | bytes 110600 | tf_op jit(solution)/shard_map/ppermute | solution.py:17
  52.7 1.3 %collective-permute-start.5 = (bf16[8,48,48]{2,1,0:T(8,128)(2,1)S(1)}, bf16[8,48,48]{2,1,0:T(8,128)(2,1)S(1)}, u32[]{:S(2)}, u32[]{:S(2)}) collective-permute-start(bf16[8,48,48]{2,1,0:T(8,128)(2,1)S(1)} %get-tuple-element.30), channel_id=1, source_target_pairs={{2,0},{4,2},{6,4},{8,6},{10,8},{12,10},{14,12},{3,1},{5,3},{7,5},{... | collective-permute-start | bytes 110600 | tf_op jit(solution)/shard_map/ppermute | solution.py:18
  54.0 1.1 %collective-permute-done.4 = bf16[8,48,48]{2,1,0:T(8,128)(2,1)S(1)} collective-permute-done((bf16[8,48,48]{2,1,0:T(8,128)(2,1)S(1)}, bf16[8,48,48]{2,1,0:T(8,128)(2,1)S(1)}, u32[]{:S(2)}, u32[]{:S(2)}) %collective-permute-start.4) | collective-permute-done | bytes 36896 | tf_op jit(solution)/shard_map/ppermute | solution.py:17
  55.0 4.2 %collective-permute-done.5 = bf16[8,48,48]{2,1,0:T(8,128)(2,1)S(1)} collective-permute-done((bf16[8,48,48]{2,1,0:T(8,128)(2,1)S(1)}, bf16[8,48,48]{2,1,0:T(8,128)(2,1)S(1)}, u32[]{:S(2)}, u32[]{:S(2)}) %collective-permute-start.5) | collective-permute-done | bytes 36896 | tf_op jit(solution)/shard_map/ppermute | solution.py:18
  59.2 1.3 %collective-permute-start.6 = (bf16[28,8,48]{2,1,0:T(8,128)(2,1)S(1)}, bf16[28,8,48]{2,1,0:T(8,128)(2,1)S(1)}, u32[]{:S(2)}, u32[]{:S(2)}) collective-permute-start(bf16[28,8,48]{2,1,0:T(8,128)(2,1)S(1)} %get-tuple-element.14), channel_id=1, source_target_pairs={{0,1},{2,3},{4,5},{6,7},{8,9},{10,11},{12,13},{14,15},{16,17},{18,... | collective-permute-start | bytes 64520 | tf_op jit(solution)/shard_map/ppermute | solution.py:17
  60.5 1.3 %collective-permute-start.7 = (bf16[28,8,48]{2,1,0:T(8,128)(2,1)S(1)}, bf16[28,8,48]{2,1,0:T(8,128)(2,1)S(1)}, u32[]{:S(2)}, u32[]{:S(2)}) collective-permute-start(bf16[28,8,48]{2,1,0:T(8,128)(2,1)S(1)} %get-tuple-element.15), channel_id=1, source_target_pairs={{1,0},{3,2},{5,4},{7,6},{9,8},{11,10},{13,12},{15,14},{17,16},{19,... | collective-permute-start | bytes 64520 | tf_op jit(solution)/shard_map/ppermute | solution.py:18
  61.8 1.8 %collective-permute-done.7 = bf16[28,8,48]{2,1,0:T(8,128)(2,1)S(1)} collective-permute-done((bf16[28,8,48]{2,1,0:T(8,128)(2,1)S(1)}, bf16[28,8,48]{2,1,0:T(8,128)(2,1)S(1)}, u32[]{:S(2)}, u32[]{:S(2)}) %collective-permute-start.7) | collective-permute-done | bytes 21536 | tf_op jit(solution)/shard_map/ppermute | solution.py:18
  64.0 0.6 concatenate.23
  65.8 0.8 reshape.35
  66.6 6.0 %all-to-all-start = ((bf16[8,2,1728]{2,1,0:T(2,128)(2,1)}), bf16[8,2,1728]{2,1,0:T(2,128)(2,1)S(1)}, u32[]{:S(2)}, u32[]{:S(2)}) async-start(bf16[8,2,1728]{2,1,0:T(2,128)(2,1)} %reshape.35), calls=%async_computation | async-start | bytes 114688 | tf_op jit(solution)/shard_map/all_to_all | solution.py:100
  72.6 6.8 %all-to-all-done = bf16[8,2,1728]{2,1,0:T(2,128)(2,1)S(1)} async-done(((bf16[8,2,1728]{2,1,0:T(2,128)(2,1)}), bf16[8,2,1728]{2,1,0:T(2,128)(2,1)S(1)}, u32[]{:S(2)}, u32[]{:S(2)}) %all-to-all-start) | async-done | bytes 55328 | tf_op jit(solution)/shard_map/all_to_all | solution.py:100
  79.9 3.8 %all_to_all.10 = bf16[2,2,6912]{2,1,0:T(2,128)(2,1)S(1)} all-to-all(bf16[2,2,6912]{2,1,0:T(2,128)(2,1)S(1)} %reshape.37), channel_id=1, replica_groups=mesh['group'=2,'row'=8,'col'=2] {'col'}, dimensions={0} | all-to-all | bytes 110592 | tf_op jit(solution)/shard_map/all_to_all | solution.py:99
  84.6 6.0 %collective-permute-done.8 = bf16[4,6,12,48]{3,0,2,1:T(4,128)(2,1)S(1)} collective-permute-done((bf16[4,6,12,48]{3,0,2,1:T(4,128)(2,1)S(1)}, bf16[4,6,12,48]{3,0,2,1:T(4,128)(2,1)S(1)}, u32[]{:S(2)}, u32[]{:S(2)}) %collective-permute-start.8) | collective-permute-done | bytes 27680 | tf_op jit(solution)/shard_map/ppermute | solution.py:26
  91.7 0.9 fusion.6
  (51 shorter events, 5.9 us)
Async XLA Ops:
  0.0 48.8 %copy-start = (bf16[3,3,48,48]{3,2,1,0:T(8,128)(2,1)S(1)}, bf16[3,3,48,48]{3,2,1,0:T(8,128)(2,1)}, u32[]{:S(2)}) copy-start(bf16[3,3,48,48]{3,2,1,0:T(8,128)(2,1)} %param.15) | copy-start | bytes 124420
  0.0 0.7 copy-start.5
  0.7 32.3 %copy-start.3 = (bf16[96,48]{0,1:T(8,128)(2,1)S(1)}, bf16[96,48]{0,1:T(8,128)(2,1)}, u32[]{:S(2)}) copy-start(bf16[96,48]{0,1:T(8,128)(2,1)} %param.13) | copy-start | bytes 27652
  0.7 32.5 %copy-start.4 = (bf16[96,48]{0,1:T(8,128)(2,1)S(1)}, bf16[96,48]{0,1:T(8,128)(2,1)}, u32[]{:S(2)}) copy-start(bf16[96,48]{0,1:T(8,128)(2,1)} %param.14) | copy-start | bytes 27652
  33.0 0.9 copy-start.1
  34.0 5.1 %collective-permute-start = (bf16[4,48,48]{2,1,0:T(8,128)(2,1)S(1)}, bf16[4,48,48]{2,1,0:T(8,128)(2,1)S(1)}, u32[]{:S(2)}, u32[]{:S(2)}) collective-permute-start(bf16[4,48,48]{2,1,0:T(8,128)(2,1)S(1)} %get-tuple-element.31), channel_id=1, source_target_pairs={{0,2},{2,4},{4,6},{6,8},{8,10},{10,12},{12,14},{1,3},{3,5},{5,7},{... | collective-permute-start | bytes 55304 | tf_op jit(solution)/shard_map/ppermute | solution.py:17
  37.4 6.0 %collective-permute-start.1 = (bf16[4,48,48]{2,1,0:T(8,128)(2,1)S(1)}, bf16[4,48,48]{2,1,0:T(8,128)(2,1)S(1)}, u32[]{:S(2)}, u32[]{:S(2)}) collective-permute-start(bf16[4,48,48]{2,1,0:T(8,128)(2,1)S(1)} %get-tuple-element.32), channel_id=1, source_target_pairs={{2,0},{4,2},{6,4},{8,6},{10,8},{12,10},{14,12},{3,1},{5,3},{7,5},{... | collective-permute-start | bytes 55304 | tf_op jit(solution)/shard_map/ppermute | solution.py:18
  43.4 2.6 %collective-permute-start.2 = (bf16[20,4,48]{2,1,0:T(4,128)(2,1)S(1)}, bf16[20,4,48]{2,1,0:T(4,128)(2,1)S(1)}, u32[]{:S(2)}, u32[]{:S(2)}) collective-permute-start(bf16[20,4,48]{2,1,0:T(4,128)(2,1)S(1)} %get-tuple-element.25), channel_id=1, source_target_pairs={{0,1},{2,3},{4,5},{6,7},{8,9},{10,11},{12,13},{14,15},{16,17},{18,... | collective-permute-start | bytes 23048 | tf_op jit(solution)/shard_map/ppermute | solution.py:17
  44.7 3.1 %collective-permute-start.3 = (bf16[20,4,48]{2,1,0:T(4,128)(2,1)S(1)}, bf16[20,4,48]{2,1,0:T(4,128)(2,1)S(1)}, u32[]{:S(2)}, u32[]{:S(2)}) collective-permute-start(bf16[20,4,48]{2,1,0:T(4,128)(2,1)S(1)} %get-tuple-element.26), channel_id=1, source_target_pairs={{1,0},{3,2},{5,4},{7,6},{9,8},{11,10},{13,12},{15,14},{17,16},{19,... | collective-permute-start | bytes 23048 | tf_op jit(solution)/shard_map/ppermute | solution.py:18
  48.8 0.7 copy-start.6
  49.8 5.2 %collective-permute-start.4 = (bf16[8,48,48]{2,1,0:T(8,128)(2,1)S(1)}, bf16[8,48,48]{2,1,0:T(8,128)(2,1)S(1)}, u32[]{:S(2)}, u32[]{:S(2)}) collective-permute-start(bf16[8,48,48]{2,1,0:T(8,128)(2,1)S(1)} %get-tuple-element.29), channel_id=1, source_target_pairs={{0,2},{2,4},{4,6},{6,8},{8,10},{10,12},{12,14},{1,3},{3,5},{5,7},{... | collective-permute-start | bytes 110600 | tf_op jit(solution)/shard_map/ppermute | solution.py:17
  52.7 6.5 %collective-permute-start.5 = (bf16[8,48,48]{2,1,0:T(8,128)(2,1)S(1)}, bf16[8,48,48]{2,1,0:T(8,128)(2,1)S(1)}, u32[]{:S(2)}, u32[]{:S(2)}) collective-permute-start(bf16[8,48,48]{2,1,0:T(8,128)(2,1)S(1)} %get-tuple-element.30), channel_id=1, source_target_pairs={{2,0},{4,2},{6,4},{8,6},{10,8},{12,10},{14,12},{3,1},{5,3},{7,5},{... | collective-permute-start | bytes 110600 | tf_op jit(solution)/shard_map/ppermute | solution.py:18
  59.2 2.6 %collective-permute-start.6 = (bf16[28,8,48]{2,1,0:T(8,128)(2,1)S(1)}, bf16[28,8,48]{2,1,0:T(8,128)(2,1)S(1)}, u32[]{:S(2)}, u32[]{:S(2)}) collective-permute-start(bf16[28,8,48]{2,1,0:T(8,128)(2,1)S(1)} %get-tuple-element.14), channel_id=1, source_target_pairs={{0,1},{2,3},{4,5},{6,7},{8,9},{10,11},{12,13},{14,15},{16,17},{18,... | collective-permute-start | bytes 64520 | tf_op jit(solution)/shard_map/ppermute | solution.py:17
  60.5 3.1 %collective-permute-start.7 = (bf16[28,8,48]{2,1,0:T(8,128)(2,1)S(1)}, bf16[28,8,48]{2,1,0:T(8,128)(2,1)S(1)}, u32[]{:S(2)}, u32[]{:S(2)}) collective-permute-start(bf16[28,8,48]{2,1,0:T(8,128)(2,1)S(1)} %get-tuple-element.15), channel_id=1, source_target_pairs={{1,0},{3,2},{5,4},{7,6},{9,8},{11,10},{13,12},{15,14},{17,16},{19,... | collective-permute-start | bytes 64520 | tf_op jit(solution)/shard_map/ppermute | solution.py:18
  64.0 0.9 copy-start.2
  64.6 0.7 copy-start.7
  66.6 12.8 %all-to-all-start = ((bf16[8,2,1728]{2,1,0:T(2,128)(2,1)}), bf16[8,2,1728]{2,1,0:T(2,128)(2,1)S(1)}, u32[]{:S(2)}, u32[]{:S(2)}) async-start(bf16[8,2,1728]{2,1,0:T(2,128)(2,1)} %reshape.35), calls=%async_computation | async-start | bytes 114688 | tf_op jit(solution)/shard_map/all_to_all | solution.py:100
  84.1 6.6 %collective-permute-start.8 = (bf16[4,6,12,48]{3,0,2,1:T(4,128)(2,1)S(1)}, bf16[4,6,12,48]{3,0,2,1:T(4,128)(2,1)S(1)}, u32[]{:S(2)}, u32[]{:S(2)}) collective-permute-start(bf16[4,6,12,48]{3,0,2,1:T(4,128)(2,1)S(1)} %get-tuple-element.28), channel_id=1, source_target_pairs={{0,8},{2,10},{4,12},{6,14},{8,0},{10,2},{12,4},{14,6},{1,9},{3,11}... | collective-permute-start | bytes 82952 | tf_op jit(solution)/shard_map/ppermute | solution.py:26
  91.0 0.7 copy-start.8
  91.0 0.7 copy-start.9
  91.0 0.7 copy-start.10
where the time goes:
time: 93.2 us; the launch traced here: 92.6 us
  blocking collectives  36.1 us (39%)
  waiting for transfers between devices  26.4 us (28%)
  starting transfers between devices  20.5 us (22%)
  local copies, waits for them, and re-layouts  7.02 us (8%)
  matrix products  1.8 us (2%)
    all_gather x1, blocking collectives, on_device(): all_bins = lax.all_gather(embedding, 'row', axis=0, tiled=True)  32.3 us
    ppermute x4, waiting for transfers between devices, padded(): after = lax.ppermute(leading, axis, down)  12 us
    ppermute x4, starting transfers between devices, padded(): before = lax.ppermute(last, axis, up)  8.8 us
    all_to_all x1, waiting for transfers between devices, on_device(): lax.all_to_all(arranged, 'row', split_axis=0, concat_axis=0, tiled=True)  6.85 us
    ppermute x1, waiting for transfers between devices, swapped(): return lax.ppermute(value, axis, pairs)  6.02 us
    all_to_all x1, starting transfers between devices, on_device(): lax.all_to_all(arranged, 'row', split_axis=0, concat_axis=0, tiled=True)  5.98 us
    ppermute x4, starting transfers between devices, padded(): after = lax.ppermute(leading, axis, down)  5.17 us
    unnamed x27, local copies, waits for them, and re-layouts  4.82 us
  transfers between devices with their start and end apart: 10, of which 8 were waited for; matrix products, arithmetic and copies ran while one was open for 0% of the time, Pallas kernels for 0%

commit v1 on v0

--- a/solution.py
+++ b/solution.py
@@ -58,7 +58,14 @@
     row_count = lax.axis_size("row")
     row_at = lax.axis_index("row")
     col_at = lax.axis_index("col")
-    all_bins = lax.all_gather(embedding, "row", axis=0, tiled=True)
+    ways, here, step = (lax.axis_size("row"), lax.axis_index("row"), embedding.shape[0])
+    line, have = (embedding, 1)
+    while have < ways:
+        line = jnp.concatenate(
+            [line, lax.ppermute(line, "row", [(d, (d - have) % ways) for d in range(ways)])], axis=0
+        )
+        have = 2 * have
+    all_bins = jnp.roll(line, here * step, axis=0)
     row_terms = jnp.dot(all_bins, w_row, preferred_element_type=jnp.float32)
     col_terms = jnp.dot(all_bins, w_col, preferred_element_type=jnp.float32)
     own_rows = lax.dynamic_slice_in_dim(row_terms, row_at * patch_rows, patch_rows, 0)

time: 93.2 us -> 80.3 us (0.86)
  blocking collectives: 36.1 us -> 3.77 us
  starting transfers between devices: 20.5 us -> 32.3 us
  waiting for transfers between devices: 26.4 us -> 33.7 us
    all_gather x1 -> x0, blocking collectives: 32.3 us -> none  [on_device(): all_bins = lax.all_gather(embedding, 'row', axis=0, tiled=True)]
    ppermute x0 -> x3, waiting for transfers between devices: none -> 8.07 us  [on_device(): lax.ppermute(line, 'row', [(d, (d - have) % ways) for d in range(ways)])]
    ppermute x0 -> x3, starting transfers between devices: none -> 7.73 us  [on_device(): lax.ppermute(line, 'row', [(d, (d - have) % ways) for d in range(ways)])]
    ppermute x4, starting transfers between devices: 8.8 us -> 12.6 us  [padded(): before = lax.ppermute(last, axis, up)]
    ppermute x4, waiting for transfers between devices: 12 us -> 10.4 us  [padded(): after = lax.ppermute(leading, axis, down)]
    unnamed x27 -> x26, local copies, waits for them, and re-layouts: 4.82 us -> 4.08 us
  transfers between devices with their start and end apart: 10 -> 13, of which waited for: 8 -> 11; matrix products, arithmetic and copies ran while one was open for 0% -> 0% of each run, Pallas kernels for 0% -> 0%
where the time goes in v1:
time: 80.3 us; the launch traced here: 79.7 us
  waiting for transfers between devices  33.7 us (42%)
  starting transfers between devices  32.3 us (40%)
  local copies, waits for them, and re-layouts  6.49 us (8%)
  blocking collectives  3.77 us (5%)
  matrix products  1.81 us (2%)
  other arithmetic  1.23 us (2%)
    ppermute x4, starting transfers between devices, padded(): before = lax.ppermute(last, axis, up)  12.6 us
    ppermute x4, waiting for transfers between devices, padded(): after = lax.ppermute(leading, axis, down)  10.4 us
    ppermute x3, waiting for transfers between devices, on_device(): lax.ppermute(line, 'row', [(d, (d - have) % ways) for d in range(ways)])  8.07 us
    ppermute x3, starting transfers between devices, on_device(): lax.ppermute(line, 'row', [(d, (d - have) % ways) for d in range(ways)])  7.73 us
    all_to_all x1, waiting for transfers between devices, on_device(): lax.all_to_all(arranged, 'row', split_axis=0, concat_axis=0, tiled=True)  6.85 us
    all_to_all x1, starting transfers between devices, on_device(): lax.all_to_all(arranged, 'row', split_axis=0, concat_axis=0, tiled=True)  6.29 us
    ppermute x1, waiting for transfers between devices, swapped(): return lax.ppermute(value, axis, pairs)  6.02 us
    ppermute x4, starting transfers between devices, padded(): after = lax.ppermute(leading, axis, down)  5.17 us
  transfers between devices with their start and end apart: 13, of which 11 were waited for; matrix products, arithmetic and copies ran while one was open for 0% of the time, Pallas kernels for 0%

profile of v1, /device:TPU:0, one launch (start us, length us, event | category | flops | bytes accessed | tf_op | source)
XLA Modules:
  0.0 79.7 jit_solution(3860093857542430630)
XLA Ops:
  0.0 6.0 %collective-permute-start = (bf16[12,96]{1,0:T(8,128)(2,1)}, bf16[12,96]{1,0:T(8,128)(2,1)S(1)}, u32[]{:S(2)}, u32[]{:S(2)}) collective-permute-start(bf16[12,96]{1,0:T(8,128)(2,1)} %param.12), channel_id=1, source_target_pairs={{0,14},{2,0},{4,2},{6,4},{8,6},{10,8},{12,10},{14,12},{1,15},{3,1}... | collective-permute-start | bytes 6920 | tf_op jit(solution)/shard_map/ppermute | solution.py:65
  6.0 1.5 %collective-permute-done = bf16[12,96]{1,0:T(8,128)(2,1)S(1)} collective-permute-done((bf16[12,96]{1,0:T(8,128)(2,1)}, bf16[12,96]{1,0:T(8,128)(2,1)S(1)}, u32[]{:S(2)}, u32[]{:S(2)}) %collective-permute-start) | collective-permute-done | bytes 2336 | tf_op jit(solution)/shard_map/ppermute | solution.py:65
  8.2 1.4 %collective-permute-start.1 = (bf16[24,96]{1,0:T(8,128)(2,1)S(1)}, bf16[24,96]{1,0:T(8,128)(2,1)S(1)}, u32[]{:S(2)}, u32[]{:S(2)}) collective-permute-start(bf16[24,96]{1,0:T(8,128)(2,1)S(1)} %pad_maximum_fusion.7), channel_id=1, source_target_pairs={{0,12},{2,14},{4,0},{6,2},{8,4},{10,6},{12,8},{14,10},{1,13},{3,15... | collective-permute-start | bytes 13832 | tf_op jit(solution)/shard_map/ppermute | solution.py:65
  9.6 2.3 %collective-permute-done.1 = bf16[24,96]{1,0:T(8,128)(2,1)S(1)} collective-permute-done((bf16[24,96]{1,0:T(8,128)(2,1)S(1)}, bf16[24,96]{1,0:T(8,128)(2,1)S(1)}, u32[]{:S(2)}, u32[]{:S(2)}) %collective-permute-start.1) | collective-permute-done | bytes 4640 | tf_op jit(solution)/shard_map/ppermute | solution.py:65
  12.3 4.3 %collective-permute-done.2 = bf16[48,96]{1,0:T(8,128)(2,1)S(1)} collective-permute-done((bf16[48,96]{1,0:T(8,128)(2,1)S(1)}, bf16[48,96]{1,0:T(8,128)(2,1)S(1)}, u32[]{:S(2)}, u32[]{:S(2)}) %collective-permute-start.2) | collective-permute-done | bytes 9248 | tf_op jit(solution)/shard_map/ppermute | solution.py:65
  17.7 5.2 %collective-permute-start.3 = (bf16[4,48,48]{2,1,0:T(8,128)(2,1)S(1)}, bf16[4,48,48]{2,1,0:T(8,128)(2,1)S(1)}, u32[]{:S(2)}, u32[]{:S(2)}) collective-permute-start(bf16[4,48,48]{2,1,0:T(8,128)(2,1)S(1)} %get-tuple-element.31), channel_id=1, source_target_pairs={{0,2},{2,4},{4,6},{6,8},{8,10},{10,12},{12,14},{1,3},{3,5},{5,7},{... | collective-permute-start | bytes 55304 | tf_op jit(solution)/shard_map/ppermute | solution.py:17
  22.9 1.3 %collective-permute-start.4 = (bf16[4,48,48]{2,1,0:T(8,128)(2,1)S(1)}, bf16[4,48,48]{2,1,0:T(8,128)(2,1)S(1)}, u32[]{:S(2)}, u32[]{:S(2)}) collective-permute-start(bf16[4,48,48]{2,1,0:T(8,128)(2,1)S(1)} %get-tuple-element.32), channel_id=1, source_target_pairs={{2,0},{4,2},{6,4},{8,6},{10,8},{12,10},{14,12},{3,1},{5,3},{7,5},{... | collective-permute-start | bytes 55304 | tf_op jit(solution)/shard_map/ppermute | solution.py:18
  24.6 4.3 %collective-permute-done.4 = bf16[4,48,48]{2,1,0:T(8,128)(2,1)S(1)} collective-permute-done((bf16[4,48,48]{2,1,0:T(8,128)(2,1)S(1)}, bf16[4,48,48]{2,1,0:T(8,128)(2,1)S(1)}, u32[]{:S(2)}, u32[]{:S(2)}) %collective-permute-start.4) | collective-permute-done | bytes 18464 | tf_op jit(solution)/shard_map/ppermute | solution.py:18
  28.9 1.3 %collective-permute-start.5 = (bf16[20,4,48]{2,1,0:T(4,128)(2,1)S(1)}, bf16[20,4,48]{2,1,0:T(4,128)(2,1)S(1)}, u32[]{:S(2)}, u32[]{:S(2)}) collective-permute-start(bf16[20,4,48]{2,1,0:T(4,128)(2,1)S(1)} %get-tuple-element.25), channel_id=1, source_target_pairs={{0,1},{2,3},{4,5},{6,7},{8,9},{10,11},{12,13},{14,15},{16,17},{18,... | collective-permute-start | bytes 23048 | tf_op jit(solution)/shard_map/ppermute | solution.py:17
  30.2 1.3 %collective-permute-start.6 = (bf16[20,4,48]{2,1,0:T(4,128)(2,1)S(1)}, bf16[20,4,48]{2,1,0:T(4,128)(2,1)S(1)}, u32[]{:S(2)}, u32[]{:S(2)}) collective-permute-start(bf16[20,4,48]{2,1,0:T(4,128)(2,1)S(1)} %get-tuple-element.26), channel_id=1, source_target_pairs={{1,0},{3,2},{5,4},{7,6},{9,8},{11,10},{13,12},{15,14},{17,16},{19,... | collective-permute-start | bytes 23048 | tf_op jit(solution)/shard_map/ppermute | solution.py:18
  31.5 1.8 %collective-permute-done.6 = bf16[20,4,48]{2,1,0:T(4,128)(2,1)S(1)} collective-permute-done((bf16[20,4,48]{2,1,0:T(4,128)(2,1)S(1)}, bf16[20,4,48]{2,1,0:T(4,128)(2,1)S(1)}, u32[]{:S(2)}, u32[]{:S(2)}) %collective-permute-start.6) | collective-permute-done | bytes 7712 | tf_op jit(solution)/shard_map/ppermute | solution.py:18
  35.3 3.1 %collective-permute-start.7 = (bf16[8,48,48]{2,1,0:T(8,128)(2,1)S(1)}, bf16[8,48,48]{2,1,0:T(8,128)(2,1)S(1)}, u32[]{:S(2)}, u32[]{:S(2)}) collective-permute-start(bf16[8,48,48]{2,1,0:T(8,128)(2,1)S(1)} %get-tuple-element.29), channel_id=1, source_target_pairs={{0,2},{2,4},{4,6},{6,8},{8,10},{10,12},{12,14},{1,3},{3,5},{5,7},{... | collective-permute-start | bytes 110600 | tf_op jit(solution)/shard_map/ppermute | solution.py:17
  38.4 1.3 %collective-permute-start.8 = (bf16[8,48,48]{2,1,0:T(8,128)(2,1)S(1)}, bf16[8,48,48]{2,1,0:T(8,128)(2,1)S(1)}, u32[]{:S(2)}, u32[]{:S(2)}) collective-permute-start(bf16[8,48,48]{2,1,0:T(8,128)(2,1)S(1)} %get-tuple-element.30), channel_id=1, source_target_pairs={{2,0},{4,2},{6,4},{8,6},{10,8},{12,10},{14,12},{3,1},{5,3},{7,5},{... | collective-permute-start | bytes 110600 | tf_op jit(solution)/shard_map/ppermute | solution.py:18
  39.7 1.1 %collective-permute-done.7 = bf16[8,48,48]{2,1,0:T(8,128)(2,1)S(1)} collective-permute-done((bf16[8,48,48]{2,1,0:T(8,128)(2,1)S(1)}, bf16[8,48,48]{2,1,0:T(8,128)(2,1)S(1)}, u32[]{:S(2)}, u32[]{:S(2)}) %collective-permute-start.7) | collective-permute-done | bytes 36896 | tf_op jit(solution)/shard_map/ppermute | solution.py:17
  40.7 4.4 %collective-permute-done.8 = bf16[8,48,48]{2,1,0:T(8,128)(2,1)S(1)} collective-permute-done((bf16[8,48,48]{2,1,0:T(8,128)(2,1)S(1)}, bf16[8,48,48]{2,1,0:T(8,128)(2,1)S(1)}, u32[]{:S(2)}, u32[]{:S(2)}) %collective-permute-start.8) | collective-permute-done | bytes 36896 | tf_op jit(solution)/shard_map/ppermute | solution.py:18
  45.1 1.3 %collective-permute-start.10 = (bf16[28,8,48]{2,1,0:T(8,128)(2,1)S(1)}, bf16[28,8,48]{2,1,0:T(8,128)(2,1)S(1)}, u32[]{:S(2)}, u32[]{:S(2)}) collective-permute-start(bf16[28,8,48]{2,1,0:T(8,128)(2,1)S(1)} %get-tuple-element.15), channel_id=1, source_target_pairs={{1,0},{3,2},{5,4},{7,6},{9,8},{11,10},{13,12},{15,14},{17,16},{19,... | collective-permute-start | bytes 64520 | tf_op jit(solution)/shard_map/ppermute | solution.py:18
  46.4 3.0 %collective-permute-start.9 = (bf16[28,8,48]{2,1,0:T(8,128)(2,1)S(1)}, bf16[28,8,48]{2,1,0:T(8,128)(2,1)S(1)}, u32[]{:S(2)}, u32[]{:S(2)}) collective-permute-start(bf16[28,8,48]{2,1,0:T(8,128)(2,1)S(1)} %get-tuple-element.14), channel_id=1, source_target_pairs={{0,1},{2,3},{4,5},{6,7},{8,9},{10,11},{12,13},{14,15},{16,17},{18,... | collective-permute-start | bytes 64520 | tf_op jit(solution)/shard_map/ppermute | solution.py:17
  49.5 0.9 %collective-permute-done.9 = bf16[28,8,48]{2,1,0:T(8,128)(2,1)S(1)} collective-permute-done((bf16[28,8,48]{2,1,0:T(8,128)(2,1)S(1)}, bf16[28,8,48]{2,1,0:T(8,128)(2,1)S(1)}, u32[]{:S(2)}, u32[]{:S(2)}) %collective-permute-start.9) | collective-permute-done | bytes 21536 | tf_op jit(solution)/shard_map/ppermute | solution.py:17
  52.5 0.8 %reshape.33 = bf16[8,2,1728]{2,1,0:T(2,128)(2,1)} reshape(bf16[8,6,12,48]{3,2,1,0:T(8,128)(2,1)S(1)} %copy.23) | data formatting | bytes 110592
  53.3 6.3 %all-to-all-start = ((bf16[8,2,1728]{2,1,0:T(2,128)(2,1)}), bf16[8,2,1728]{2,1,0:T(2,128)(2,1)S(1)}, u32[]{:S(2)}, u32[]{:S(2)}) async-start(bf16[8,2,1728]{2,1,0:T(2,128)(2,1)} %reshape.33), calls=%async_computation | async-start | bytes 114688 | tf_op jit(solution)/shard_map/all_to_all | solution.py:107
  59.6 6.8 %all-to-all-done = bf16[8,2,1728]{2,1,0:T(2,128)(2,1)S(1)} async-done(((bf16[8,2,1728]{2,1,0:T(2,128)(2,1)}), bf16[8,2,1728]{2,1,0:T(2,128)(2,1)S(1)}, u32[]{:S(2)}, u32[]{:S(2)}) %all-to-all-start) | async-done | bytes 55328 | tf_op jit(solution)/shard_map/all_to_all | solution.py:107
  66.9 3.8 %all_to_all.10 = bf16[2,2,6912]{2,1,0:T(2,128)(2,1)S(1)} all-to-all(bf16[2,2,6912]{2,1,0:T(2,128)(2,1)S(1)} %reshape.35), channel_id=1, replica_groups=mesh['group'=2,'row'=8,'col'=2] {'col'}, dimensions={0} | all-to-all | bytes 110592 | tf_op jit(solution)/shard_map/all_to_all | solution.py:106
  71.7 6.0 %collective-permute-done.11 = bf16[4,6,12,48]{3,0,2,1:T(4,128)(2,1)S(1)} collective-permute-done((bf16[4,6,12,48]{3,0,2,1:T(4,128)(2,1)S(1)}, bf16[4,6,12,48]{3,0,2,1:T(4,128)(2,1)S(1)}, u32[]{:S(2)}, u32[]{:S(2)}) %collective-permute-start.11) | collective-permute-done | bytes 27680 | tf_op jit(solution)/shard_map/ppermute | solution.py:26
  78.8 0.9 %fusion.6 = f32[12,48]{1,0:T(8,128)} fusion(f32[12,48,48]{2,1,0:T(8,128)S(1)} %reshape.29, bf16[12,48,48]{2,1,0:T(8,128)(2,1)S(1)} %fusion.4, f32[48]{0:T(128)S(1)} %copy-done.9, f32[48]{0:T(128)S(1)} %copy-done.10, bf16[48,48]{1,0:T(8,128)(2,1)S(1)} %copy-done.8), kind=kOutput, calls=%fused_computation.9 | convolution fusion | flops 2874816 | bytes 173184 | tf_op jit(solution)/shard_map/rch,hk->rck/dot_general | solution.py:126
  (58 shorter events, 9.2 us)
Async XLA Ops:
  0.0 34.3 %copy-start = (bf16[3,3,48,48]{3,2,1,0:T(8,128)(2,1)S(1)}, bf16[3,3,48,48]{3,2,1,0:T(8,128)(2,1)}, u32[]{:S(2)}) copy-start(bf16[3,3,48,48]{3,2,1,0:T(8,128)(2,1)} %param.15) | copy-start | bytes 124420
  0.0 11.8 %copy-start.3 = (bf16[12,96]{1,0:T(8,128)(2,1)S(1)}, bf16[12,96]{1,0:T(8,128)(2,1)}, u32[]{:S(2)}) copy-start(bf16[12,96]{1,0:T(8,128)(2,1)} %param.12) | copy-start | bytes 6916
  0.0 7.5 %collective-permute-start = (bf16[12,96]{1,0:T(8,128)(2,1)}, bf16[12,96]{1,0:T(8,128)(2,1)S(1)}, u32[]{:S(2)}, u32[]{:S(2)}) collective-permute-start(bf16[12,96]{1,0:T(8,128)(2,1)} %param.12), channel_id=1, source_target_pairs={{0,14},{2,0},{4,2},{6,4},{8,6},{10,8},{12,10},{14,12},{1,15},{3,1}... | collective-permute-start | bytes 6920 | tf_op jit(solution)/shard_map/ppermute | solution.py:65
  8.2 3.6 %collective-permute-start.1 = (bf16[24,96]{1,0:T(8,128)(2,1)S(1)}, bf16[24,96]{1,0:T(8,128)(2,1)S(1)}, u32[]{:S(2)}, u32[]{:S(2)}) collective-permute-start(bf16[24,96]{1,0:T(8,128)(2,1)S(1)} %pad_maximum_fusion.7), channel_id=1, source_target_pairs={{0,12},{2,14},{4,0},{6,2},{8,4},{10,6},{12,8},{14,10},{1,13},{3,15... | collective-permute-start | bytes 13832 | tf_op jit(solution)/shard_map/ppermute | solution.py:65
  11.9 4.7 %collective-permute-start.2 = (bf16[48,96]{1,0:T(8,128)(2,1)S(1)}, bf16[48,96]{1,0:T(8,128)(2,1)S(1)}, u32[]{:S(2)}, u32[]{:S(2)}) collective-permute-start(bf16[48,96]{1,0:T(8,128)(2,1)S(1)} %pad_maximum_fusion.6), channel_id=1, source_target_pairs={{0,8},{2,10},{4,12},{6,14},{8,0},{10,2},{12,4},{14,6},{1,9},{3,11}... | collective-permute-start | bytes 27656 | tf_op jit(solution)/shard_map/ppermute | solution.py:65
  12.3 4.5 %copy-start.4 = (bf16[96,48]{0,1:T(8,128)(2,1)S(1)}, bf16[96,48]{0,1:T(8,128)(2,1)}, u32[]{:S(2)}) copy-start(bf16[96,48]{0,1:T(8,128)(2,1)} %param.13) | copy-start | bytes 27652
  12.3 5.4 %copy-start.1 = (bf16[12,48,48]{2,1,0:T(8,128)(2,1)S(1)}, bf16[12,48,48]{2,1,0:T(8,128)(2,1)}, u32[]{:S(2)}) copy-start(bf16[12,48,48]{2,1,0:T(8,128)(2,1)} %param.11) | copy-start | bytes 165892
  16.7 0.7 copy-start.5
  17.7 6.9 %collective-permute-start.3 = (bf16[4,48,48]{2,1,0:T(8,128)(2,1)S(1)}, bf16[4,48,48]{2,1,0:T(8,128)(2,1)S(1)}, u32[]{:S(2)}, u32[]{:S(2)}) collective-permute-start(bf16[4,48,48]{2,1,0:T(8,128)(2,1)S(1)} %get-tuple-element.31), channel_id=1, source_target_pairs={{0,2},{2,4},{4,6},{6,8},{8,10},{10,12},{12,14},{1,3},{3,5},{5,7},{... | collective-permute-start | bytes 55304 | tf_op jit(solution)/shard_map/ppermute | solution.py:17
  22.9 6.0 %collective-permute-start.4 = (bf16[4,48,48]{2,1,0:T(8,128)(2,1)S(1)}, bf16[4,48,48]{2,1,0:T(8,128)(2,1)S(1)}, u32[]{:S(2)}, u32[]{:S(2)}) collective-permute-start(bf16[4,48,48]{2,1,0:T(8,128)(2,1)S(1)} %get-tuple-element.32), channel_id=1, source_target_pairs={{2,0},{4,2},{6,4},{8,6},{10,8},{12,10},{14,12},{3,1},{5,3},{7,5},{... | collective-permute-start | bytes 55304 | tf_op jit(solution)/shard_map/ppermute | solution.py:18
  28.9 2.6 %collective-permute-start.5 = (bf16[20,4,48]{2,1,0:T(4,128)(2,1)S(1)}, bf16[20,4,48]{2,1,0:T(4,128)(2,1)S(1)}, u32[]{:S(2)}, u32[]{:S(2)}) collective-permute-start(bf16[20,4,48]{2,1,0:T(4,128)(2,1)S(1)} %get-tuple-element.25), channel_id=1, source_target_pairs={{0,1},{2,3},{4,5},{6,7},{8,9},{10,11},{12,13},{14,15},{16,17},{18,... | collective-permute-start | bytes 23048 | tf_op jit(solution)/shard_map/ppermute | solution.py:17
  30.2 3.1 %collective-permute-start.6 = (bf16[20,4,48]{2,1,0:T(4,128)(2,1)S(1)}, bf16[20,4,48]{2,1,0:T(4,128)(2,1)S(1)}, u32[]{:S(2)}, u32[]{:S(2)}) collective-permute-start(bf16[20,4,48]{2,1,0:T(4,128)(2,1)S(1)} %get-tuple-element.26), channel_id=1, source_target_pairs={{1,0},{3,2},{5,4},{7,6},{9,8},{11,10},{13,12},{15,14},{17,16},{19,... | collective-permute-start | bytes 23048 | tf_op jit(solution)/shard_map/ppermute | solution.py:18
  34.3 0.7 copy-start.6
  35.3 5.5 %collective-permute-start.7 = (bf16[8,48,48]{2,1,0:T(8,128)(2,1)S(1)}, bf16[8,48,48]{2,1,0:T(8,128)(2,1)S(1)}, u32[]{:S(2)}, u32[]{:S(2)}) collective-permute-start(bf16[8,48,48]{2,1,0:T(8,128)(2,1)S(1)} %get-tuple-element.29), channel_id=1, source_target_pairs={{0,2},{2,4},{4,6},{6,8},{8,10},{10,12},{12,14},{1,3},{3,5},{5,7},{... | collective-permute-start | bytes 110600 | tf_op jit(solution)/shard_map/ppermute | solution.py:17
  38.4 6.8 %collective-permute-start.8 = (bf16[8,48,48]{2,1,0:T(8,128)(2,1)S(1)}, bf16[8,48,48]{2,1,0:T(8,128)(2,1)S(1)}, u32[]{:S(2)}, u32[]{:S(2)}) collective-permute-start(bf16[8,48,48]{2,1,0:T(8,128)(2,1)S(1)} %get-tuple-element.30), channel_id=1, source_target_pairs={{2,0},{4,2},{6,4},{8,6},{10,8},{12,10},{14,12},{3,1},{5,3},{7,5},{... | collective-permute-start | bytes 110600 | tf_op jit(solution)/shard_map/ppermute | solution.py:18
  45.1 4.3 %collective-permute-start.10 = (bf16[28,8,48]{2,1,0:T(8,128)(2,1)S(1)}, bf16[28,8,48]{2,1,0:T(8,128)(2,1)S(1)}, u32[]{:S(2)}, u32[]{:S(2)}) collective-permute-start(bf16[28,8,48]{2,1,0:T(8,128)(2,1)S(1)} %get-tuple-element.15), channel_id=1, source_target_pairs={{1,0},{3,2},{5,4},{7,6},{9,8},{11,10},{13,12},{15,14},{17,16},{19,... | collective-permute-start | bytes 64520 | tf_op jit(solution)/shard_map/ppermute | solution.py:18
  46.4 3.9 %collective-permute-start.9 = (bf16[28,8,48]{2,1,0:T(8,128)(2,1)S(1)}, bf16[28,8,48]{2,1,0:T(8,128)(2,1)S(1)}, u32[]{:S(2)}, u32[]{:S(2)}) collective-permute-start(bf16[28,8,48]{2,1,0:T(8,128)(2,1)S(1)} %get-tuple-element.14), channel_id=1, source_target_pairs={{0,1},{2,3},{4,5},{6,7},{8,9},{10,11},{12,13},{14,15},{16,17},{18,... | collective-permute-start | bytes 64520 | tf_op jit(solution)/shard_map/ppermute | solution.py:17
  50.7 0.9 %copy-start.2 = (bf16[3,3,48,48]{3,2,1,0:T(8,128)(2,1)S(1)}, bf16[3,3,48,48]{3,2,1,0:T(8,128)(2,1)}, u32[]{:S(2)}) copy-start(bf16[3,3,48,48]{3,2,1,0:T(8,128)(2,1)} %param.17) | copy-start | bytes 124420
  51.4 0.7 copy-start.7
  53.3 13.1 %all-to-all-start = ((bf16[8,2,1728]{2,1,0:T(2,128)(2,1)}), bf16[8,2,1728]{2,1,0:T(2,128)(2,1)S(1)}, u32[]{:S(2)}, u32[]{:S(2)}) async-start(bf16[8,2,1728]{2,1,0:T(2,128)(2,1)} %reshape.33), calls=%async_computation | async-start | bytes 114688 | tf_op jit(solution)/shard_map/all_to_all | solution.py:107
  71.1 6.6 %collective-permute-start.11 = (bf16[4,6,12,48]{3,0,2,1:T(4,128)(2,1)S(1)}, bf16[4,6,12,48]{3,0,2,1:T(4,128)(2,1)S(1)}, u32[]{:S(2)}, u32[]{:S(2)}) collective-permute-start(bf16[4,6,12,48]{3,0,2,1:T(4,128)(2,1)S(1)} %get-tuple-element.28), channel_id=1, source_target_pairs={{0,8},{2,10},{4,12},{6,14},{8,0},{10,2},{12,4},{14,6},{1,9},{3,11}... | collective-permute-start | bytes 82952 | tf_op jit(solution)/shard_map/ppermute | solution.py:26
  78.0 0.7 copy-start.8
  78.1 0.7 copy-start.9
  78.1 0.7 copy-start.10
